TPU v7x, 32 devices: a whole 2x2x4 slice. The times are simulated.
32 devices in a mesh: copies: 2 (over y), blk: 4 (over x, core), virt: 4 (over z).
Axes of the slice: x: 2, y: 2, z: 4, core: 2. Of those that a mesh axis runs over, the one named last changes fastest.
Arguments:
- three_index: bfloat16 [32, 512, 2048], P(('copies', 'blk'), 'virt'), parts along dimension 0, may hold values from -0.59765625 to 0.59765625
- occ_energy: float32 [32], P(('copies', 'blk')), parts along dimension 0, may hold values from -2 to -0.5
- virt_energy: float32 [1024], P('copies'), parts along dimension 0, may hold values from 0.3 to 3
Outputs:
- gradient: bfloat16 [32, 512, 2048], P(('copies', 'blk'), 'virt'), parts along dimension 0
There are 2 independent parts, one for each index of `copies`. A program takes and returns all parts, laid end to end along the dimension named above; each array names one. Nothing has to cross between parts.
All inputs are finite; a program needn't handle non-finite values.
Results may differ from a plain program's by a relative error of at most 0.0055.
Values may be sent and summed in bfloat16 or wider, within the bound.
A program may use at most 64 MiB of HBM per device.

v0:
```python
import jax
import jax.numpy as jnp
from jax import lax
from jax.sharding import PartitionSpec as P


def shifted(shard, axis, by):
    devices = lax.axis_size(axis)
    return lax.ppermute(shard, axis, [(i, (i + by) % devices) for i in range(devices)])


def contract(left, right):
    return lax.dot_general(
        left, right, (((1,), (1,)), ((), ())), preferred_element_type=jnp.float32
    )


def pair_block(
    own_rows,
    part_full,
    part_rows,
    own_full,
    energy_own,
    energy_part,
    energy_rows,
    virt_energy,
    diagonal,
):
    occ_count, rows_here, aux_count = own_rows.shape
    virt_count = part_full.shape[1]
    first = contract(
        own_rows.reshape(occ_count * rows_here, aux_count),
        part_full.reshape(occ_count * virt_count, aux_count),
    )
    first = first.reshape(occ_count, rows_here, occ_count, virt_count)
    if diagonal:
        second = first.transpose(2, 1, 0, 3)
    else:
        second = contract(
            part_rows.reshape(occ_count * rows_here, aux_count),
            own_full.reshape(occ_count * virt_count, aux_count),
        )
        second = second.reshape(occ_count, rows_here, occ_count, virt_count).transpose(2, 1, 0, 3)
    denom = (
        energy_own[:, None, None, None]
        + energy_part[None, None, :, None]
        - energy_rows[None, :, None, None]
        - virt_energy[None, None, None, :]
    )
    tbar = ((2.0 * first - second) / denom).astype(jnp.bfloat16)
    flat = tbar.reshape(occ_count * rows_here, occ_count * virt_count)
    own = jnp.dot(
        flat,
        part_full.reshape(occ_count * virt_count, aux_count),
        preferred_element_type=jnp.float32,
    )
    return (tbar, first, own.reshape(occ_count, rows_here, aux_count))


def local(three_index, occ_energy, virt_energy):
    occ_count, rows_here, aux_count = three_index.shape
    virt_count = virt_energy.shape[0]
    row_start = lax.axis_index("virt") * rows_here
    energy_rows = lax.dynamic_slice_in_dim(virt_energy, row_start, rows_here, 0)
    own_full = lax.all_gather(three_index, "virt", axis=1, tiled=True)
    part_full, energy_part = (
        shifted(own_full, "blk", 1),
        shifted(occ_energy.astype(jnp.bfloat16), "blk", 1).astype(occ_energy.dtype),
    )
    part_rows = lax.dynamic_slice_in_dim(part_full, row_start, rows_here, 1)
    unused_tbar, unused_first, diag_own = pair_block(
        three_index,
        own_full,
        three_index,
        own_full,
        occ_energy,
        occ_energy,
        energy_rows,
        virt_energy,
        True,
    )
    tbar, first, cross_own = pair_block(
        three_index,
        part_full,
        part_rows,
        own_full,
        occ_energy,
        energy_part,
        energy_rows,
        virt_energy,
        False,
    )
    tiles = lax.all_to_all(tbar, "virt", split_axis=3, concat_axis=1, tiled=True)
    partial_value = lax.dot_general(
        tiles.reshape(occ_count * virt_count, occ_count * rows_here),
        own_full.reshape(occ_count * virt_count, aux_count),
        (((0,), (0,)), ((), ())),
        preferred_element_type=jnp.float32,
    )
    summed = partial_value.reshape(occ_count, rows_here, aux_count).astype(jnp.bfloat16)
    partner = shifted(summed, "blk", -1)
    return (diag_own + cross_own + partner.astype(jnp.float32)).astype(jnp.bfloat16)


def solution(mesh):
    placed = (P(("copies", "blk"), "virt", None), P(("copies", "blk")), P("copies"))
    return jax.shard_map(
        local,
        mesh=mesh,
        in_specs=placed,
        out_specs=P(("copies", "blk"), "virt", None),
        check_vma=False,
    )
```

profile of v0, /device:TPU:0, one launch (start us, length us, event | category | flops | bytes accessed | tf_op | source)
XLA Modules:
  0.0 382.2 jit_solution(1829108738289670631)
XLA Ops:
  6.5 0.0 all-gather.2.cloned.1.call-start
  6.5 0.7 all-gather.2.cloned.1.call-update
  7.3 154.0 %all-gather.2.cloned.1.call-done = bf16[4,512,2048]{2,1,0:T(8,128)(2,1)} async-done(((bf16[4,128,2048]{2,1,0:T(8,128)(2,1)}), bf16[4,512,2048]{2,1,0:T(8,128)(2,1)}) %all-gather.2.cloned.1.call-update) | async-done | bytes 8388624 | tf_op jit(solution)/shard_map/all_gather | solution.py:65
  161.3 0.0 collective-permute-start
  161.3 0.7 convert_element_type.22
  161.9 1.6 collective-permute-start.1
  163.5 0.8 dynamic_slice.6
  164.3 90.2 %collective-permute-done.1 = bf16[4]{0:T(256)(128)(2,1)S(1)} collective-permute-done((bf16[4]{0:T(256)(128)(2,1)S(1)}, bf16[4]{0:T(256)(128)(2,1)S(1)}, u32[]{:S(2)}, u32[]{:S(2)}) %collective-permute-start.1) | collective-permute-done | bytes 40 | tf_op jit(solution)/shard_map/ppermute | solution.py:9
  254.5 0.8 broadcast_add_fusion
  255.3 0.0 slice-start
  255.3 0.1 broadcast_subtract_fusion
  255.3 0.0 slice-start.1
  255.3 0.0 copy-start.3
  255.3 0.0 collective-permute-done
  255.4 7.9 %fusion.2 = f32[4,128,4,512]{3,1,0,2:T(8,128)S(1)} fusion(bf16[4,512,2048]{2,1,0:T(8,128)(2,1)} %collective-permute-done, bf16[4,128,2048]{2,1,0:T(8,128)(2,1)} %param.3), kind=kOutput, calls=%fused_computation.2 | convolution fusion | flops 4294967296 | bytes 14680064 | tf_op jit(solution)/shard_map/dot_general | solution.py:13
  263.2 0.0 slice-done
  263.3 0.0 slice-done.1
  263.3 0.0 copy-done.3
  263.3 6.9 %fusion.13 = bf16[4,128,4,512]{3,1,0,2:T(8,128)(2,1)S(1)} fusion(f32[4,128,4,512]{3,1,0,2:T(8,128)S(1)} %fusion.2, bf16[4,512,2048]{2,1,0:T(8,128)(2,1)S(1)} %bitcast.76, f32[4,128,4]{1,0,2:T(4,128)S(1)} %get-tuple-element.5, bf16[4,512,2048]{2,1,0:T(8,128)(2,1)} %collective-permute-done, s32[]{:T(128)S(6)} %select_n.4, f32[512]{0:T(512)S(1)} %copy-done.3), kind=kOutput, calls=%fused_computation.15 | convolution fusion | flops 4300210176 | bytes 16787460 | tf_op jit(solution)/shard_map/dot_general | solution.py:13
  270.2 0.0 copy-start.1
  270.2 1.3 copy-done.1
  271.5 3.1 copy.16
  274.6 51.3 %all_to_all.15 = bf16[4,128,4,512]{1,0,2,3:T(4,128)(2,1)S(1)} all-to-all(bf16[4,128,4,512]{1,0,2,3:T(4,128)(2,1)} %copy.16), channel_id=1, replica_groups=mesh['copies'=2,'blk'=4,'virt'=4] {'virt'}, dimensions={3} | all-to-all | bytes 4194304 | tf_op jit(solution)/shard_map/all_to_all | solution.py:93
  325.9 3.1 copy.17
  329.0 2.0 copy.30
  330.9 2.4 copy.18
  333.3 0.0 copy-start
  333.3 8.7 %convolution_convert_fusion = bf16[4,128,2048]{2,1,0:T(8,128)(2,1)S(1)} fusion(bf16[4,128,2048]{2,1,0:T(8,128)(2,1)} %bitcast.73, bf16[2048,2048,1]{1,0,2:T(8,128)(2,1)} %bitcast.74), kind=kOutput, calls=%fused_computation.20 | convolution fusion | flops 4296015872 | bytes 12582912 | tf_op jit(solution)/shard_map/dot_general | solution.py:94
  342.0 0.2 collective-permute-start.2
  342.2 0.0 copy-done
  342.2 7.0 %fusion.8 = f32[4,128,4,512]{3,1,2,0:T(8,128)S(1)} fusion(bf16[4,512,2048]{2,1,0:T(8,128)(2,1)} %all-gather.2.cloned.1.call-done, bf16[4,128,2048]{2,1,0:T(8,128)(2,1)S(1)} %copy-done), kind=kOutput, calls=%fused_computation.8 | convolution fusion | flops 4294967296 | bytes 14680064 | tf_op jit(solution)/shard_map/dot_general | solution.py:13
  349.2 0.0 copy-start.2
  349.2 7.5 %fusion.4 = f32[4,128,2048,1]{2,1,0,3:T(8,128)S(1)} fusion(bf16[4,512,2048]{2,1,0:T(8,128)(2,1)} %all-gather.2.cloned.1.call-done, f32[4,128,4,512]{3,1,2,0:T(8,128)S(1)} %fusion.8, f32[512]{0:T(512)S(1)} %copy-done.3, f32[4,128,4]{1,0,2:T(4,128)S(1)} %get-tuple-element.6), kind=kOutput, calls=%fused_computation.4 | convolution fusion | flops 4300210176 | bytes 16787456 | tf_op jit(solution)/shard_map/dot_general | solution.py:52
  356.7 9.1 %collective-permute-done.2 = bf16[4,128,2048]{2,1,0:T(8,128)(2,1)S(1)} collective-permute-done((bf16[4,128,2048]{2,1,0:T(8,128)(2,1)S(1)}, bf16[4,128,2048]{2,1,0:T(8,128)(2,1)S(1)}, u32[]{:S(2)}, u32[]{:S(2)}) %collective-permute-start.2) | collective-permute-done | bytes 2097184 | tf_op jit(solution)/shard_map/ppermute | solution.py:9
  365.8 0.0 copy-done.2
  365.8 9.6 %fusion.11 = bf16[4,128,2048]{2,1,0:T(8,128)(2,1)} fusion(f32[4,128,2048,1]{2,1,0,3:T(8,128)S(1)} %fusion.4, bf16[4,128,2048]{2,1,0:T(8,128)(2,1)S(1)} %collective-permute-done.2, bf16[4,128,4,512]{3,1,0,2:T(8,128)(2,1)S(1)} %copy-done.2, bf16[4,512,2048]{2,1,0:T(8,128)(2,1)} %collective-permute-done), kind=kOutput, calls=%fused_computation.12 | convolution fusion | flops 4299161600 | bytes 18874368 | tf_op jit(solution)/shard_map/dot_general | solution.py:52
  (2 shorter events, 0.0 us)
Async XLA Ops:
  6.5 154.7 %all-gather.2.cloned.1.call-start = ((), (), s32[]{:S(2)}) async-start(), calls=%async_computation.1 | async-start | bytes 10485760 | tf_op jit(solution)/shard_map/all_gather | solution.py:65
  161.3 94.1 %collective-permute-start = (bf16[4,512,2048]{2,1,0:T(8,128)(2,1)}, bf16[4,512,2048]{2,1,0:T(8,128)(2,1)}, u32[]{:S(2)}, u32[]{:S(2)}) collective-permute-start(bf16[4,512,2048]{2,1,0:T(8,128)(2,1)} %all-gather.2.cloned.1.call-done), channel_id=1, source_target_pairs={{0,4},{4,8},{8,12},{12,0},{1,5},{5,9},{9,13},{13,1},{2,6},{6,10},{... | collective-permute-start | bytes 25165832 | tf_op jit(solution)/shard_map/ppermute | solution.py:9
  161.9 92.5 %collective-permute-start.1 = (bf16[4]{0:T(256)(128)(2,1)S(1)}, bf16[4]{0:T(256)(128)(2,1)S(1)}, u32[]{:S(2)}, u32[]{:S(2)}) collective-permute-start(bf16[4]{0:T(256)(128)(2,1)S(1)} %convert_element_type.22), channel_id=1, source_target_pairs={{0,4},{4,8},{8,12},{12,0},{1,5},{5,9},{9,13},{13,1},{2,6},{6,10},{... | collective-permute-start | bytes 32 | tf_op jit(solution)/shard_map/ppermute | solution.py:9
  255.3 8.0 %slice-start = ((s8[8388608]{0:T(1024)(128)(4,1)}), s8[4194304]{0:T(1024)(128)(4,1)S(1)}, s32[]{:S(2)}) async-start(s8[8388608]{0:T(1024)(128)(4,1)} %bitcast.75), calls=%async_computation.2 | async-start | bytes 8388608
  255.3 7.9 %slice-start.1 = ((s8[8388608]{0:T(1024)(128)(4,1)}), s8[4194304]{0:T(1024)(128)(4,1)S(1)}, s32[]{:S(2)}) async-start(s8[8388608]{0:T(1024)(128)(4,1)} %bitcast.75), calls=%async_computation.3 | async-start | bytes 8388608
  255.3 7.9 %copy-start.3 = (f32[512]{0:T(512)S(1)}, f32[512]{0:T(512)}, u32[]{:S(2)}) copy-start(f32[512]{0:T(512)} %param.5) | copy-start | bytes 6148
  270.2 1.3 copy-start.1
  333.3 8.9 %copy-start = (bf16[4,128,2048]{2,1,0:T(8,128)(2,1)S(1)}, bf16[4,128,2048]{2,1,0:T(8,128)(2,1)}, u32[]{:S(2)}) copy-start(bf16[4,128,2048]{2,1,0:T(8,128)(2,1)} %param.3) | copy-start | bytes 6291460
  342.0 23.8 %collective-permute-start.2 = (bf16[4,128,2048]{2,1,0:T(8,128)(2,1)S(1)}, bf16[4,128,2048]{2,1,0:T(8,128)(2,1)S(1)}, u32[]{:S(2)}, u32[]{:S(2)}) collective-permute-start(bf16[4,128,2048]{2,1,0:T(8,128)(2,1)S(1)} %convolution_convert_fusion), channel_id=1, source_target_pairs={{0,12},{4,0},{8,4},{12,8},{1,13},{5,1},{9,5},{13,9},{2,14},{6,2},{... | collective-permute-start | bytes 6291464 | tf_op jit(solution)/shard_map/ppermute | solution.py:9
  349.2 16.6 %copy-start.2 = (bf16[4,128,4,512]{3,1,0,2:T(8,128)(2,1)S(1)}, bf16[4,128,4,512]{3,1,0,2:T(8,128)(2,1)}, u32[]{:S(2)}) copy-start(bf16[4,128,4,512]{3,1,0,2:T(8,128)(2,1)} %copy-done.1) | copy-start | bytes 6291460
Sparse Core Ops, SparseCore 0:
  8.9 152.3 all-gather.1
where the time goes:
time: 383 us; the launch traced here: 382 us
  waiting for transfers between devices  254 us (66%)
  blocking collectives  51.3 us (13%)
  matrix products  47.5 us (12%)
  between operations  13.5 us (4%)
  local copies, waits for them, and re-layouts  12.6 us (3%)
    all_gather x1, waiting for transfers between devices, local(): own_full = lax.all_gather(three_index, 'virt', axis=1, tiled=True)  154 us
    ppermute x3, waiting for transfers between devices, shifted(): lax.ppermute(shard, axis, [(i, (i + by) % devices) for i in range(devices)])  99.3 us
    all_to_all x1, blocking collectives, local(): lax.all_to_all(tbar, 'virt', split_axis=3, concat_axis=1, tiled=True)  51.3 us
    dot_general x3, matrix products, contract(): lax.dot_general(left, right, (((1,), (1,)), ((), ())), preferred_element_...  21.7 us
    dot_general x2, matrix products, pair_block(): jnp.dot(flat, part_full.reshape(occ_count * virt_count, aux_count), prefe...  17.1 us
    dot_general x1, matrix products, local(): lax.dot_general(tiles.reshape(occ_count * virt_count, occ_count * rows_he...  8.65 us
  transfers between devices with their start and end apart: 4, of which 3 were waited for; matrix products, arithmetic and copies ran while one was open for 4% of the time, Pallas kernels for 0%

commit v1 on v0

v1 whole, which is shorter than its diff:
```python
import functools

import jax
import jax.numpy as jnp
from jax import lax
from jax.experimental import pallas as pl
from jax.experimental.pallas import tpu as pltpu
from jax.sharding import PartitionSpec as P

MESH = pl.DeviceIdType.MESH
SEND_COLUMNS = 256
SUM_COLUMNS = 512


def shifted(shard, axis, by):
    devices = lax.axis_size(axis)
    return lax.ppermute(shard, axis, [(i, (i + by) % devices) for i in range(devices)])


def contract(left, right):
    return lax.dot_general(
        left, right, (((1,), (1,)), ((), ())), preferred_element_type=jnp.float32
    )


def plain_local(three_index, occ_energy, virt_energy):
    occ, rows, aux = three_index.shape
    virt = virt_energy.shape[0]
    energy_rows = lax.dynamic_slice_in_dim(virt_energy, lax.axis_index("virt") * rows, rows, 0)
    part_rows = shifted(three_index, "blk", 1)
    own_full = lax.all_gather(three_index, "virt", axis=1, tiled=True)
    part_full = shifted(own_full, "blk", 1)
    energy_part = shifted(occ_energy, "blk", 1)

    def pairs(left, right):
        both = contract(left.reshape(occ * rows, aux), right.reshape(occ * virt, aux))
        return both.reshape(occ, rows, occ, virt)

    def denominator(left, right):
        return (
            left[:, None, None, None]
            + right[None, None, :, None]
            - energy_rows[None, :, None, None]
            - virt_energy[None, None, None, :]
        )

    def spread(tbar, full):
        return jnp.dot(
            tbar.astype(jnp.bfloat16).reshape(occ * rows, occ * virt),
            full.reshape(occ * virt, aux),
            preferred_element_type=jnp.float32,
        ).reshape(occ, rows, aux)

    diag = pairs(three_index, own_full)
    first = pairs(three_index, part_full)
    second = pairs(part_rows, own_full)
    own = spread(
        (2.0 * diag - diag.transpose(2, 1, 0, 3)) / denominator(occ_energy, occ_energy), own_full
    )
    own += spread(
        (2.0 * first - second.transpose(2, 1, 0, 3)) / denominator(occ_energy, energy_part),
        part_full,
    )
    partner = spread(
        (2.0 * second - first.transpose(2, 1, 0, 3)) / denominator(energy_part, occ_energy),
        own_full,
    ).astype(jnp.bfloat16)
    partner = shifted(partner, "blk", -1)
    return (own + partner.astype(jnp.float32)).astype(jnp.bfloat16)


def kernel(
    members,
    blocks,
    a_ref,
    e_ref,
    column_ref,
    row_ref,
    o_ref,
    own_full,
    part_full,
    e_part,
    acc,
    pacc,
    psend,
    precv,
    k_ref,
    x_ref,
    tu_ref,
    t_ref,
    send_up,
    send_down,
    send_next,
    recv_own,
    recv_part,
    send_back,
    recv_back,
    e_sems,
    local_sem,
):
    occ, rows, aux = a_ref.shape
    size = occ * rows
    v = lax.axis_index("virt")
    g = lax.axis_index("blk")
    after = lax.rem(g + 1, blocks)
    before = lax.rem(g + blocks - 1, blocks)
    has_up = v + 1 < members
    has_down = v > 0

    def copy_up(src, s, c):
        return pltpu.make_async_remote_copy(
            src_ref=src, dst_ref=own_full.at[s, c], send_sem=send_up.at[s, c],
            recv_sem=recv_own.at[s, c], device_id={"virt": v + 1}, device_id_type=MESH,
        )

    def copy_down(src, s, c):
        return pltpu.make_async_remote_copy(
            src_ref=src, dst_ref=own_full.at[s, c], send_sem=send_down.at[s, c],
            recv_sem=recv_own.at[s, c], device_id={"virt": v - 1}, device_id_type=MESH,
        )

    def copy_next(src, s, c):
        return pltpu.make_async_remote_copy(
            src_ref=src, dst_ref=part_full.at[s, c], send_sem=send_next.at[s, c],
            recv_sem=recv_part.at[s, c], device_id={"blk": after}, device_id_type=MESH,
        )

    def arrived_own(s, c):
        return pltpu.make_async_remote_copy(
            src_ref=own_full.at[s, c], dst_ref=own_full.at[s, c], send_sem=send_next.at[s, c],
            recv_sem=recv_own.at[s, c], device_id={"blk": after}, device_id_type=MESH,
        )

    def copy_back(k):
        return pltpu.make_async_remote_copy(
            src_ref=psend.at[k], dst_ref=precv.at[k], send_sem=send_back.at[k],
            recv_sem=recv_back.at[k], device_id={"blk": before}, device_id_type=MESH,
        )

    energy_copy = pltpu.make_async_remote_copy(
        src_ref=e_ref, dst_ref=e_part, send_sem=e_sems.at[0], recv_sem=e_sems.at[1],
        device_id={"blk": after}, device_id_type=MESH,
    )
    keep = pltpu.make_async_copy(a_ref, own_full.at[v], local_sem)

    barrier = pltpu.get_barrier_semaphore()
    pl.semaphore_signal(barrier, inc=1, device_id={"blk": after}, device_id_type=MESH)
    pl.semaphore_signal(barrier, inc=1, device_id={"blk": before}, device_id_type=MESH)

    @pl.when(has_up)
    def _():
        pl.semaphore_signal(barrier, inc=1, device_id={"virt": v + 1}, device_id_type=MESH)

    @pl.when(has_down)
    def _():
        pl.semaphore_signal(barrier, inc=1, device_id={"virt": v - 1}, device_id_type=MESH)

    pl.semaphore_wait(barrier, 2 + has_up.astype(jnp.int32) + has_down.astype(jnp.int32))

    energy_copy.start()
    for c in range(occ):
        @pl.when(has_up)
        def _():
            copy_up(a_ref.at[c], v, c).start()

        @pl.when(has_down)
        def _():
            copy_down(a_ref.at[c], v, c).start()

        copy_next(a_ref.at[c], v, c).start()
    keep.start()
    acc[...] = jnp.zeros_like(acc)
    pacc[...] = jnp.zeros_like(pacc)
    keep.wait()
    energy_copy.wait_recv()

    def inverse(left, i, right, j, s):
        own_rows = column_ref[pl.ds(pl.multiple_of(v * rows, rows), rows), :]
        return 1.0 / ((left[i : i + 1, 0:1] + right[j : j + 1, 0:1]) - own_rows - row_ref[s])

    def at(i):
        return slice(i * rows, (i + 1) * rows)

    def add_columns(total, left, source, s, width):
        @pl.loop(0, aux // width)
        def _(k):
            cols = pl.ds(pl.multiple_of(k * width, width), width)
            total[:, cols] += jnp.dot(
                left[...], source[s, :, :, cols].reshape(size, width),
                preferred_element_type=jnp.float32,
            )

    last = jnp.where(2 * v > members - 1, 0, members - 1)

    def compute(s):
        own = own_full[s].reshape(size, aux)
        k_ref[...] = contract(a_ref[...].reshape(size, aux), own)
        for i in range(occ):
            for j in range(occ):
                tu_ref[at(i), at(j)] = (
                    (2.0 * k_ref[at(i), at(j)] - k_ref[at(j), at(i)])
                    * inverse(e_ref, i, e_ref, j, s)
                ).astype(jnp.bfloat16)
        add_columns(acc, tu_ref, own_full, s, SUM_COLUMNS)

        @pl.when(s == v)
        def _():
            for c in range(occ):
                copy_next(part_full.at[s, c], s, c).wait_recv()

        k_ref[...] = contract(part_full[v].reshape(size, aux), own_full[s].reshape(size, aux))

        @pl.when(s != v)
        def _():
            for c in range(occ):
                copy_next(part_full.at[s, c], s, c).wait_recv()

        x_ref[...] = contract(a_ref[...].reshape(size, aux), part_full[s].reshape(size, aux))
        for i in range(occ):
            for j in range(occ):
                scale = inverse(e_ref, i, e_part, j, s)
                x = x_ref[at(i), at(j)]
                y = k_ref[at(j), at(i)]
                t_ref[at(i), at(j)] = ((2.0 * x - y) * scale).astype(jnp.bfloat16)
                tu_ref[at(j), at(i)] = ((2.0 * y - x) * scale).astype(jnp.bfloat16)

        @pl.when(s != last)
        def _():
            add_columns(pacc, tu_ref, own_full, s, SUM_COLUMNS)
            add_columns(acc, t_ref, part_full, s, SUM_COLUMNS)

    def level(d, carry):
        @pl.when(d > 0)
        def _():
            for c in range(occ):
                below, above = v - d, v + d

                @pl.when(below >= 0)
                def _():
                    arrived_own(below, c).wait_recv()

                    @pl.when(has_up)
                    def _():
                        copy_up(own_full.at[below, c], below, c).start()

                    copy_next(own_full.at[below, c], below, c).start()

                @pl.when(above < members)
                def _():
                    arrived_own(above, c).wait_recv()

                    @pl.when(has_down)
                    def _():
                        copy_down(own_full.at[above, c], above, c).start()

                    copy_next(own_full.at[above, c], above, c).start()

        def side(t, inner):
            s = v - d + 2 * d * t

            @pl.when((s >= 0) & (s < members) & (d + (1 - t) > 0))
            def _():
                compute(s)

            return inner

        return lax.fori_loop(0, 2, side, carry)

    lax.fori_loop(0, members, level, 0)

    for k in range(aux // SEND_COLUMNS):
        cols = slice(k * SEND_COLUMNS, (k + 1) * SEND_COLUMNS)
        psend[k] = (
            pacc[:, cols]
            + jnp.dot(
                tu_ref[...], own_full[last, :, :, cols].reshape(size, SEND_COLUMNS),
                preferred_element_type=jnp.float32,
            )
        ).astype(jnp.bfloat16)
        copy_back(k).start()
    add_columns(acc, t_ref, part_full, last, SUM_COLUMNS)
    for k in range(aux // SEND_COLUMNS):
        cols = slice(k * SEND_COLUMNS, (k + 1) * SEND_COLUMNS)
        copy_back(k).wait_recv()
        o_ref[:, :, cols] = (
            (acc[:, cols] + precv[k].astype(jnp.float32))
            .astype(jnp.bfloat16)
            .reshape(occ, rows, SEND_COLUMNS)
        )

    energy_copy.wait_send()
    for k in range(aux // SEND_COLUMNS):
        copy_back(k).wait_send()

    def drain(s, carry):
        for c in range(occ):
            copy_next(own_full.at[s, c], s, c).wait_send()

            @pl.when(has_up & (s <= v))
            def _():
                copy_up(own_full.at[s, c], s, c).wait_send()

            @pl.when(has_down & (s >= v))
            def _():
                copy_down(own_full.at[s, c], s, c).wait_send()

        return carry

    lax.fori_loop(0, members, drain, 0)


def fused_local(three_index, occ_energy, virt_energy):
    occ, rows, aux = three_index.shape
    members, blocks = lax.axis_size("virt"), lax.axis_size("blk")
    size, parts = occ * rows, aux // SEND_COLUMNS
    energies = jnp.broadcast_to(occ_energy[:, None], (occ, 128))
    vmem = pl.BlockSpec(memory_space=pltpu.VMEM)
    dma = pltpu.SemaphoreType.DMA
    return pl.pallas_call(
        functools.partial(kernel, members, blocks),
        out_shape=jax.ShapeDtypeStruct((occ, rows, aux), jnp.bfloat16),
        in_specs=[vmem] * 4,
        out_specs=vmem,
        scratch_shapes=[
            pltpu.VMEM((members, occ, rows, aux), jnp.bfloat16),
            pltpu.VMEM((members, occ, rows, aux), jnp.bfloat16),
            pltpu.VMEM((occ, 128), jnp.float32),
            pltpu.VMEM((size, aux), jnp.float32),
            pltpu.VMEM((size, aux), jnp.float32),
            pltpu.VMEM((parts, size, SEND_COLUMNS), jnp.bfloat16),
            pltpu.VMEM((parts, size, SEND_COLUMNS), jnp.bfloat16),
            pltpu.VMEM((size, size), jnp.float32),
            pltpu.VMEM((size, size), jnp.float32),
            pltpu.VMEM((size, size), jnp.bfloat16),
            pltpu.VMEM((size, size), jnp.bfloat16),
            dma((members, occ)),
            dma((members, occ)),
            dma((members, occ)),
            dma((members, occ)),
            dma((members, occ)),
            dma((parts,)),
            dma((parts,)),
            dma((2,)),
            dma,
        ],
        compiler_params=pltpu.CompilerParams(
            collective_id=0, has_side_effects=True, vmem_limit_bytes=62 * 2**20
        ),
    )(
        three_index,
        energies,
        virt_energy[:, None],
        virt_energy.reshape(members, 1, rows),
    )


def local(three_index, occ_energy, virt_energy):
    occ, rows, aux = three_index.shape
    if rows % 128 == 0 and aux % SUM_COLUMNS == 0:
        return fused_local(three_index, occ_energy, virt_energy)
    return plain_local(three_index, occ_energy, virt_energy)


def solution(mesh):
    placed = (P(("copies", "blk"), "virt", None), P(("copies", "blk")), P("copies"))
    return jax.shard_map(
        local,
        mesh=mesh,
        in_specs=placed,
        out_specs=P(("copies", "blk"), "virt", None),
        check_vma=False,
    )
```

time: 383 us -> 184 us (0.48)
  waiting for transfers between devices: 254 us -> 0 us
  Pallas kernels: 0 us -> 176 us
  blocking collectives: 51.3 us -> 0 us
  matrix products: 47.5 us -> 0 us
  between operations: 13.5 us -> 0.01 us
  local copies, waits for them, and re-layouts: 12.6 us -> 6.01 us
    pallas_call x0 -> x1, Pallas kernels: none -> 176 us  [fused_local(): pl.pallas_call(functools.partial(kernel, members, blocks), out_shape=jax....]
    all_gather x1 -> x0, waiting for transfers between devices: 154 us -> none  [local(): own_full = lax.all_gather(three_index, 'virt', axis=1, tiled=True)]
    ppermute x3 -> x0, waiting for transfers between devices: 99.3 us -> none  [shifted(): lax.ppermute(shard, axis, [(i, (i + by) % devices) for i in range(devices)])]
    all_to_all x1 -> x0, blocking collectives: 51.3 us -> none  [local(): lax.all_to_all(tbar, 'virt', split_axis=3, concat_axis=1, tiled=True)]
    dot_general x6 -> x0, matrix products: 47.5 us -> none  [the longest x3 21.7 us: contract(): lax.dot_general(left, right, (((1,), (1,)), ((), ())), preferred_element_...]
  transfers between devices with their start and end apart: 4 -> 0, of which waited for: 3 -> 0; matrix products, arithmetic and copies ran while one was open for 4% -> 0% of each run, Pallas kernels for 0% -> 0%
where the time goes in v1:
time: 184 us; the launch traced here: 182 us
  Pallas kernels  176 us (96%)
  local copies, waits for them, and re-layouts  6.01 us (3%)
    pallas_call x1, Pallas kernels, fused_local(): pl.pallas_call(functools.partial(kernel, members, blocks), out_shape=jax....  176 us

profile of v1, /device:TPU:0, one launch (start us, length us, event | category | flops | bytes accessed | tf_op | source)
XLA Modules:
  0.0 182.1 jit_solution(8752175701200842532)
XLA Ops:
  0.0 1.3 broadcast_in_dim.4.e_ref
  1.3 1.5 copy.4.column_ref
  2.9 176.1 %shard_map.37 = bf16[4,128,2048]{2,1,0:T(8,128)(2,1)} custom-call(bf16[4,128,2048]{2,1,0:T(8,128)(2,1)} %a_ref.1, f32[4,128]{1,0:T(4,128)} %broadcast_in_dim.4.e_ref, f32[512,1]{1,0:T(8,128)} %copy.4.column_ref, f32[4,1,128]{2,1,0:T(1,128)} %bitcast.3), custom_call_target="tpu_custom_call" | custom-call | tf_op jit(solution)/shard_map/pallas_call | solution.py:319
  179.0 3.2 %copy.6 = bf16[4,128,2048]{2,1,0:T(8,128)(2,1)} copy(bf16[4,128,2048]{2,1,0:T(8,128)(2,1)} %shard_map.37) | data formatting | bytes 4194304

commit v2 on v1

v2 whole, which is shorter than its diff:
```python
import functools

import jax
import jax.numpy as jnp
from jax import lax
from jax.experimental import pallas as pl
from jax.experimental.pallas import tpu as pltpu
from jax.sharding import PartitionSpec as P

MESH = pl.DeviceIdType.MESH
SEND_COLUMNS = 256
SUM_COLUMNS = 512


def shifted(shard, axis, by):
    devices = lax.axis_size(axis)
    return lax.ppermute(shard, axis, [(i, (i + by) % devices) for i in range(devices)])


def contract(left, right):
    return lax.dot_general(
        left, right, (((1,), (1,)), ((), ())), preferred_element_type=jnp.float32
    )


def plain_local(three_index, occ_energy, virt_energy):
    occ, rows, aux = three_index.shape
    virt = virt_energy.shape[0]
    energy_rows = lax.dynamic_slice_in_dim(virt_energy, lax.axis_index("virt") * rows, rows, 0)
    part_rows = shifted(three_index, "blk", 1)
    own_full = lax.all_gather(three_index, "virt", axis=1, tiled=True)
    part_full = shifted(own_full, "blk", 1)
    energy_part = shifted(occ_energy, "blk", 1)

    def pairs(left, right):
        both = contract(left.reshape(occ * rows, aux), right.reshape(occ * virt, aux))
        return both.reshape(occ, rows, occ, virt)

    def denominator(left, right):
        return (
            left[:, None, None, None]
            + right[None, None, :, None]
            - energy_rows[None, :, None, None]
            - virt_energy[None, None, None, :]
        )

    def spread(tbar, full):
        return jnp.dot(
            tbar.astype(jnp.bfloat16).reshape(occ * rows, occ * virt),
            full.reshape(occ * virt, aux),
            preferred_element_type=jnp.float32,
        ).reshape(occ, rows, aux)

    diag = pairs(three_index, own_full)
    first = pairs(three_index, part_full)
    second = pairs(part_rows, own_full)
    own = spread(
        (2.0 * diag - diag.transpose(2, 1, 0, 3)) / denominator(occ_energy, occ_energy), own_full
    )
    own += spread(
        (2.0 * first - second.transpose(2, 1, 0, 3)) / denominator(occ_energy, energy_part),
        part_full,
    )
    partner = spread(
        (2.0 * second - first.transpose(2, 1, 0, 3)) / denominator(energy_part, occ_energy),
        own_full,
    ).astype(jnp.bfloat16)
    partner = shifted(partner, "blk", -1)
    return (own + partner.astype(jnp.float32)).astype(jnp.bfloat16)


def kernel(
    blocks,
    a_ref,
    e_ref,
    row_ref,
    o_ref,
    own_full,
    part_full,
    e_part,
    column_ref,
    acc,
    pacc,
    racc,
    psend,
    precv,
    hsend,
    hrecv,
    rsend,
    rrecv,
    k_ref,
    x_ref,
    tu_ref,
    t_ref,
    send_in,
    send_out,
    send_next,
    recv_own,
    recv_part,
    back_sems,
    help_sems,
    result_sems,
    e_sems,
    local_sem,
):
    occ, rows, aux = a_ref.shape
    size = occ * rows
    half = occ // 2
    chunks = range(aux // SEND_COLUMNS)
    v = lax.axis_index("virt")
    g = lax.axis_index("blk")
    after = lax.rem(g + 1, blocks)
    before = lax.rem(g + blocks - 1, blocks)
    step = jnp.where(v < 2, 1, -1)
    middle = (v == 1) | (v == 2)
    end = (v == 0) | (v == 3)
    inner = v + step
    outer = lax.rem(v - step + 4, 4)
    far = lax.rem(v + 2 * step + 4, 4)
    near = jnp.where(middle, outer, inner)
    last = jnp.where(middle, inner, far)

    def remote(src, dst, send, recv, **where):
        return pltpu.make_async_remote_copy(
            src_ref=src, dst_ref=dst, send_sem=send, recv_sem=recv,
            device_id=where, device_id_type=MESH,
        )

    def to_inner(s, c):
        return remote(
            own_full.at[s, c], own_full.at[s, c], send_in.at[s, c], recv_own.at[s, c], virt=inner
        )

    def to_outer(s, c):
        return remote(
            own_full.at[s, c], own_full.at[s, c], send_out.at[s, c], recv_own.at[s, c], virt=outer
        )

    def to_next(s, c):
        return remote(
            own_full.at[s, c], part_full.at[s, c], send_next.at[s, c], recv_part.at[s, c],
            blk=after,
        )

    def back(k):
        return remote(
            psend.at[k], precv.at[k], back_sems.at[0, k], back_sems.at[1, k], blk=before
        )

    def help_back(k):
        return remote(
            hsend.at[k], hrecv.at[k], help_sems.at[0, k], help_sems.at[1, k], blk=before
        )

    def result(k):
        return remote(
            rsend.at[k], rrecv.at[k], result_sems.at[0, k], result_sems.at[1, k], virt=outer
        )

    def own_copy(make, send, c):
        return remote(
            a_ref.at[c], make.at[v, c], send.at[v, c],
            (recv_part if make is part_full else recv_own).at[v, c],
            **({"blk": after} if make is part_full else {"virt": inner if send is send_in else outer}),
        )

    energy_copy = remote(e_ref, e_part, e_sems.at[0], e_sems.at[1], blk=after)
    keep = pltpu.make_async_copy(a_ref, own_full.at[v], local_sem)

    barrier = pltpu.get_barrier_semaphore()
    pl.semaphore_signal(barrier, inc=1, device_id={"blk": after}, device_id_type=MESH)
    pl.semaphore_signal(barrier, inc=1, device_id={"blk": before}, device_id_type=MESH)
    pl.semaphore_signal(barrier, inc=1, device_id={"virt": inner}, device_id_type=MESH)

    @pl.when(middle)
    def _():
        pl.semaphore_signal(barrier, inc=1, device_id={"virt": outer}, device_id_type=MESH)

    pl.semaphore_wait(barrier, 3 + middle.astype(jnp.int32))

    for c in range(half):
        own_copy(own_full, send_in, c).start()
    for c in range(half, occ):
        @pl.when(end)
        def _():
            own_copy(own_full, send_in, c).start()
    for c in range(occ):
        @pl.when(middle)
        def _():
            own_copy(own_full, send_out, c).start()
    energy_copy.start()
    for c in range(occ):
        own_copy(part_full, send_next, c).start()
    keep.start()
    for s in range(4):
        column_ref[s] = jnp.transpose(jnp.broadcast_to(row_ref[s], (rows, rows)))[:, 0:1]
    keep.wait()

    def inverse(left, i, right, j, r, s):
        return 1.0 / (
            (left[0:1, i : i + 1] + right[0:1, j : j + 1]) - column_ref[r] - row_ref[s]
        )

    def at(i):
        return slice(i * rows, (i + 1) * rows)

    def product(left, source, s, cols, width):
        return jnp.dot(
            left[...], source[s, :, :, cols].reshape(size, width),
            preferred_element_type=jnp.float32,
        )

    def add_columns(total, left, source, s, first):
        @pl.loop(0, aux // SUM_COLUMNS)
        def _(k):
            cols = pl.ds(pl.multiple_of(k * SUM_COLUMNS, SUM_COLUMNS), SUM_COLUMNS)
            value = product(left, source, s, cols, SUM_COLUMNS)
            if first:
                total[:, cols] = value
            else:
                total[:, cols] += value

    def shard(source, s):
        return source[s].reshape(size, aux)

    def part_arrives(s):
        for c in range(occ):
            to_next(s, c).wait_recv()

    def diagonal(r, s, total, first):
        k_ref[...] = contract(shard(own_full, r), shard(own_full, s))
        for i in range(occ):
            for j in range(occ):
                tu_ref[at(i), at(j)] = (
                    (2.0 * k_ref[at(i), at(j)] - k_ref[at(j), at(i)])
                    * inverse(e_ref, i, e_ref, j, r, s)
                ).astype(jnp.bfloat16)
        add_columns(total, tu_ref, own_full, s, first)

    def cross(r, s, same):
        if same:
            part_arrives(s)
        k_ref[...] = contract(shard(part_full, r), shard(own_full, s))
        if same is False:
            part_arrives(s)
        x_ref[...] = contract(shard(own_full, r), shard(part_full, s))
        amplitudes(r, s)

    def amplitudes(r, s):
        for i in range(occ):
            for j in range(occ):
                scale = inverse(e_ref, i, e_part, j, r, s)
                x = x_ref[at(i), at(j)]
                y = k_ref[at(j), at(i)]
                t_ref[at(i), at(j)] = ((2.0 * x - y) * scale).astype(jnp.bfloat16)
                tu_ref[at(j), at(i)] = ((2.0 * y - x) * scale).astype(jnp.bfloat16)

    def spread(s, first):
        add_columns(pacc, tu_ref, own_full, s, first)
        add_columns(acc, t_ref, part_full, s, False)

    def from_outer(c):
        to_outer(outer, c).wait_recv()
        to_inner(outer, c).start()
        to_next(outer, c).start()

    def from_partner(c, forward):
        to_inner(inner, c).wait_recv()
        to_outer(inner, c).start()
        if forward:
            to_next(inner, c).start()

    def from_far(c):
        to_inner(far, c).wait_recv()
        to_next(far, c).start()

    def from_inner(s, c):
        to_inner(s, c).wait_recv()
        to_next(s, c).start()

    diagonal(v, v, acc, True)
    energy_copy.wait_recv()

    for c in range(half):
        @pl.when(middle)
        def _():
            from_outer(c)
            from_partner(c, False)

        @pl.when(end)
        def _():
            from_inner(inner, c)

    cross(v, v, True)
    spread(v, True)

    for c in range(half, occ):
        @pl.when(middle)
        def _():
            from_outer(c)

        @pl.when(end)
        def _():
            from_inner(inner, c)

    @pl.when(middle)
    def _():
        for c in range(half, occ):
            own_copy(own_full, send_in, c).start()
        for c in range(half):
            from_far(c)

    diagonal(v, near, acc, False)

    @pl.when(middle)
    def _():
        for c in range(half, occ - 1):
            from_far(c)

    cross(v, near, False)
    spread(near, False)

    @pl.when(middle)
    def _():
        from_far(occ - 1)
        for c in range(half):
            to_next(inner, c).start()
        diagonal(outer, far, racc, True)
        cross(outer, far, False)
        for k in chunks:
            cols = slice(k * SEND_COLUMNS, (k + 1) * SEND_COLUMNS)
            hsend[k] = product(tu_ref, own_full, far, cols, SEND_COLUMNS).astype(jnp.bfloat16)
            help_back(k).start()
        for c in range(half, occ - 1):
            from_partner(c, True)
        add_columns(racc, t_ref, part_full, far, False)
        from_partner(occ - 1, True)
        for k in chunks:
            cols = slice(k * SEND_COLUMNS, (k + 1) * SEND_COLUMNS)
            help_back(k).wait_recv()
            rsend[k] = (racc[:, cols] + hrecv[k].astype(jnp.float32)).astype(jnp.bfloat16)
            result(k).start()
        diagonal(v, far, acc, False)
        cross(v, far, None)
        spread(far, False)

    @pl.when(end)
    def _():
        for c in range(occ):
            from_inner(far, c)

    diagonal(v, last, acc, False)
    cross(v, last, False)
    for k in chunks:
        cols = slice(k * SEND_COLUMNS, (k + 1) * SEND_COLUMNS)
        psend[k] = (
            pacc[:, cols] + product(tu_ref, own_full, last, cols, SEND_COLUMNS)
        ).astype(jnp.bfloat16)
        back(k).start()
    add_columns(acc, t_ref, part_full, last, False)
    for k in chunks:
        cols = slice(k * SEND_COLUMNS, (k + 1) * SEND_COLUMNS)

        @pl.when(end)
        def _():
            result(k).wait_recv()
            acc[:, cols] += rrecv[k].astype(jnp.float32)

        back(k).wait_recv()
        o_ref[:, :, cols] = (
            (acc[:, cols] + precv[k].astype(jnp.float32))
            .astype(jnp.bfloat16)
            .reshape(occ, rows, SEND_COLUMNS)
        )

    energy_copy.wait_send()
    for k in chunks:
        back(k).wait_send()
    for c in range(occ):
        for s in (v, inner, far):
            to_next(s, c).wait_send()
        to_inner(v, c).wait_send()

        @pl.when(middle)
        def _():
            to_next(outer, c).wait_send()
            to_inner(outer, c).wait_send()
            to_outer(v, c).wait_send()
            to_outer(inner, c).wait_send()

    @pl.when(middle)
    def _():
        for k in chunks:
            help_back(k).wait_send()
            result(k).wait_send()


def fused_local(three_index, occ_energy, virt_energy):
    occ, rows, aux = three_index.shape
    members, blocks = lax.axis_size("virt"), lax.axis_size("blk")
    size, parts = occ * rows, aux // SEND_COLUMNS
    vmem = pl.BlockSpec(memory_space=pltpu.VMEM)
    dma = pltpu.SemaphoreType.DMA
    full = pltpu.VMEM((members, occ, rows, aux), jnp.bfloat16)
    total = pltpu.VMEM((size, aux), jnp.float32)
    pieces = pltpu.VMEM((parts, size, SEND_COLUMNS), jnp.bfloat16)
    return pl.pallas_call(
        functools.partial(kernel, blocks),
        out_shape=jax.ShapeDtypeStruct((occ, rows, aux), jnp.bfloat16),
        in_specs=[vmem] * 3,
        out_specs=vmem,
        scratch_shapes=[
            full,
            full,
            pltpu.VMEM((1, occ), jnp.float32),
            pltpu.VMEM((members, rows, 1), jnp.float32),
            *[total] * 3,
            *[pieces] * 6,
            *[pltpu.VMEM((size, size), jnp.float32)] * 2,
            *[pltpu.VMEM((size, size), jnp.bfloat16)] * 2,
            *[dma((members, occ))] * 5,
            *[dma((2, parts))] * 3,
            dma((2,)),
            dma,
        ],
        compiler_params=pltpu.CompilerParams(
            collective_id=0, has_side_effects=True, vmem_limit_bytes=63 * 2**20
        ),
    )(three_index, occ_energy.reshape(1, occ), virt_energy.reshape(members, 1, rows))


def local(three_index, occ_energy, virt_energy):
    occ, rows, aux = three_index.shape
    tiles = rows % 128 == 0 and aux % SUM_COLUMNS == 0 and occ % 2 == 0
    if tiles and lax.axis_size("virt") == 4:
        return fused_local(three_index, occ_energy, virt_energy)
    return plain_local(three_index, occ_energy, virt_energy)


def solution(mesh):
    placed = (P(("copies", "blk"), "virt", None), P(("copies", "blk")), P("copies"))
    return jax.shard_map(
        local,
        mesh=mesh,
        in_specs=placed,
        out_specs=P(("copies", "blk"), "virt", None),
        check_vma=False,
    )
```

time: 184 us -> 161 us (0.88)
  Pallas kernels: 176 us -> 158 us
  local copies, waits for them, and re-layouts: 6.01 us -> 3.16 us
    pallas_call x1, Pallas kernels: 176 us -> 158 us  [fused_local(): pl.pallas_call(functools.partial(kernel, blocks), out_shape=jax.ShapeDtyp...]
    broadcast_in_dim x2 -> x0, local copies, waits for them, and re-layouts: 2.85 us -> none  [the longest x1 1.53 us: fused_local(): virt_energy[:, None]]
where the time goes in v2:
time: 161 us
  Pallas kernels  158 us (98%)
  local copies, waits for them, and re-layouts  3.16 us (2%)
    pallas_call x1, Pallas kernels, fused_local(): pl.pallas_call(functools.partial(kernel, blocks), out_shape=jax.ShapeDtyp...  158 us

profile of v2, /device:TPU:0, one launch (start us, length us, event | category | flops | bytes accessed | tf_op | source)
XLA Modules:
  0.0 160.9 jit_solution(6133825257424280766)
XLA Ops:
  0.0 157.8 %shard_map.37 = bf16[4,128,2048]{2,1,0:T(8,128)(2,1)} custom-call(bf16[4,128,2048]{2,1,0:T(8,128)(2,1)} %a_ref.1, f32[1,4]{1,0:T(1,128)} %bitcast.3, f32[4,1,128]{2,1,0:T(1,128)} %bitcast.2), custom_call_target="tpu_custom_call" | custom-call | tf_op jit(solution)/shard_map/pallas_call | solution.py:407
  157.8 3.2 %copy.5 = bf16[4,128,2048]{2,1,0:T(8,128)(2,1)} copy(bf16[4,128,2048]{2,1,0:T(8,128)(2,1)} %shard_map.37) | data formatting | bytes 4194304

commit v3 on v2

--- a/solution.py
+++ b/solution.py
@@ -90,8 +90,10 @@
     rrecv,
     k_ref,
     x_ref,
+    td_ref,
     tu_ref,
     t_ref,
+    staged,
     send_in,
     send_out,
     send_next,
@@ -101,6 +103,7 @@
     help_sems,
     result_sems,
     e_sems,
+    out_sems,
     local_sem,
 ):
     occ, rows, aux = a_ref.shape
@@ -164,6 +167,10 @@
             **({"blk": after} if make is part_full else {"virt": inner if send is send_in else outer}),
         )
 
+    def write(k):
+        cols = slice(k * SEND_COLUMNS, (k + 1) * SEND_COLUMNS)
+        return pltpu.make_async_copy(staged.at[k], o_ref.at[:, :, cols], out_sems.at[k])
+
     energy_copy = remote(e_ref, e_part, e_sems.at[0], e_sems.at[1], blk=after)
     keep = pltpu.make_async_copy(a_ref, own_full.at[v], local_sem)
 
@@ -227,14 +234,17 @@
         for c in range(occ):
             to_next(s, c).wait_recv()
 
-    def diagonal(r, s, total, first):
+    def pair_ratio(r, s, ratio_ref):
         k_ref[...] = contract(shard(own_full, r), shard(own_full, s))
         for i in range(occ):
             for j in range(occ):
-                tu_ref[at(i), at(j)] = (
+                ratio_ref[at(i), at(j)] = (
                     (2.0 * k_ref[at(i), at(j)] - k_ref[at(j), at(i)])
                     * inverse(e_ref, i, e_ref, j, r, s)
                 ).astype(jnp.bfloat16)
+
+    def diagonal(r, s, total, first):
+        pair_ratio(r, s, tu_ref)
         add_columns(total, tu_ref, own_full, s, first)
 
     def cross(r, s, same):
@@ -325,7 +335,7 @@
         from_far(occ - 1)
         for c in range(half):
             to_next(inner, c).start()
-        diagonal(outer, far, racc, True)
+        pair_ratio(outer, far, td_ref)
         cross(outer, far, False)
         for k in chunks:
             cols = slice(k * SEND_COLUMNS, (k + 1) * SEND_COLUMNS)
@@ -333,14 +343,21 @@
             help_back(k).start()
         for c in range(half, occ - 1):
             from_partner(c, True)
-        add_columns(racc, t_ref, part_full, far, False)
+
+        @pl.loop(0, aux // SUM_COLUMNS)
+        def _(k):
+            cols = pl.ds(pl.multiple_of(k * SUM_COLUMNS, SUM_COLUMNS), SUM_COLUMNS)
+            racc[:, cols] = product(td_ref, own_full, far, cols, SUM_COLUMNS) + product(
+                t_ref, part_full, far, cols, SUM_COLUMNS
+            )
+
+        diagonal(v, far, acc, False)
         from_partner(occ - 1, True)
         for k in chunks:
             cols = slice(k * SEND_COLUMNS, (k + 1) * SEND_COLUMNS)
             help_back(k).wait_recv()
             rsend[k] = (racc[:, cols] + hrecv[k].astype(jnp.float32)).astype(jnp.bfloat16)
             result(k).start()
-        diagonal(v, far, acc, False)
         cross(v, far, None)
         spread(far, False)
 
@@ -367,15 +384,17 @@
             acc[:, cols] += rrecv[k].astype(jnp.float32)
 
         back(k).wait_recv()
-        o_ref[:, :, cols] = (
+        staged[k] = (
             (acc[:, cols] + precv[k].astype(jnp.float32))
             .astype(jnp.bfloat16)
             .reshape(occ, rows, SEND_COLUMNS)
         )
+        write(k).start()
 
     energy_copy.wait_send()
     for k in chunks:
         back(k).wait_send()
+        write(k).wait()
     for c in range(occ):
         for s in (v, inner, far):
             to_next(s, c).wait_send()
@@ -407,8 +426,8 @@
     return pl.pallas_call(
         functools.partial(kernel, blocks),
         out_shape=jax.ShapeDtypeStruct((occ, rows, aux), jnp.bfloat16),
-        in_specs=[vmem] * 3,
-        out_specs=vmem,
+        in_specs=[pl.BlockSpec(memory_space=pl.ANY), vmem, vmem],
+        out_specs=pl.BlockSpec(memory_space=pl.ANY),
         scratch_shapes=[
             full,
             full,
@@ -417,10 +436,12 @@
             *[total] * 3,
             *[pieces] * 6,
             *[pltpu.VMEM((size, size), jnp.float32)] * 2,
-            *[pltpu.VMEM((size, size), jnp.bfloat16)] * 2,
+            *[pltpu.VMEM((size, size), jnp.bfloat16)] * 3,
+            pltpu.VMEM((parts, occ, rows, SEND_COLUMNS), jnp.bfloat16),
             *[dma((members, occ))] * 5,
             *[dma((2, parts))] * 3,
             dma((2,)),
+            dma((parts,)),
             dma,
         ],
         compiler_params=pltpu.CompilerParams(

time: 161 us -> 160 us (level)
  Pallas kernels: 158 us -> 156 us
where the time goes in v3:
time: 160 us
  Pallas kernels  156 us (98%)
  local copies, waits for them, and re-layouts  3.16 us (2%)
    pallas_call x1, Pallas kernels, fused_local(): pl.pallas_call(functools.partial(kernel, blocks), out_shape=jax.ShapeDtyp...  156 us

profile of v3, /device:TPU:0, one launch (start us, length us, event | category | flops | bytes accessed | tf_op | source)
XLA Modules:
  0.0 159.7 jit_solution(13333886916550102973)
XLA Ops:
  0.0 156.5 %shard_map.37 = bf16[4,128,2048]{2,1,0:T(8,128)(2,1)} custom-call(bf16[4,128,2048]{2,1,0:T(8,128)(2,1)} %a_ref.1, f32[1,4]{1,0:T(1,128)} %bitcast.3, f32[4,1,128]{2,1,0:T(1,128)} %bitcast.2), custom_call_target="tpu_custom_call" | custom-call | tf_op jit(solution)/shard_map/pallas_call | solution.py:426
  156.5 3.2 %copy.5 = bf16[4,128,2048]{2,1,0:T(8,128)(2,1)} copy(bf16[4,128,2048]{2,1,0:T(8,128)(2,1)} %shard_map.37) | data formatting | bytes 4194304

commit v4 on v3

--- a/solution.py
+++ b/solution.py
@@ -97,6 +97,7 @@
     send_in,
     send_out,
     send_next,
+    send_part,
     recv_own,
     recv_part,
     back_sems,
@@ -108,7 +109,8 @@
 ):
     occ, rows, aux = a_ref.shape
     size = occ * rows
-    half = occ // 2
+    cuts = 2 * occ
+    ahead = 3
     chunks = range(aux // SEND_COLUMNS)
     v = lax.axis_index("virt")
     g = lax.axis_index("blk")
@@ -116,6 +118,7 @@
     before = lax.rem(g + blocks - 1, blocks)
     step = jnp.where(v < 2, 1, -1)
     middle = (v == 1) | (v == 2)
+    even = lax.rem(g, 2) == 0
     end = (v == 0) | (v == 3)
     inner = v + step
     outer = lax.rem(v - step + 4, 4)
@@ -129,22 +132,33 @@
             device_id=where, device_id_type=MESH,
         )
 
+    def piece(ref, *lead):
+        *lead, c = lead
+        cols = slice((c % 2) * (aux // 2), (c % 2 + 1) * (aux // 2))
+        return ref.at[(*lead, c // 2, slice(None), cols)]
+
     def to_inner(s, c):
         return remote(
-            own_full.at[s, c], own_full.at[s, c], send_in.at[s, c], recv_own.at[s, c], virt=inner
+            piece(own_full, s, c), piece(own_full, s, c), send_in.at[s, c], recv_own.at[s, c], virt=inner
         )
 
     def to_outer(s, c):
         return remote(
-            own_full.at[s, c], own_full.at[s, c], send_out.at[s, c], recv_own.at[s, c], virt=outer
+            piece(own_full, s, c), piece(own_full, s, c), send_out.at[s, c], recv_own.at[s, c], virt=outer
         )
 
     def to_next(s, c):
         return remote(
-            own_full.at[s, c], part_full.at[s, c], send_next.at[s, c], recv_part.at[s, c],
+            piece(own_full, s, c), piece(part_full, s, c), send_next.at[s, c], recv_part.at[s, c],
             blk=after,
         )
 
+    def part_to_inner(c):
+        return remote(
+            piece(part_full, v, c), piece(part_full, v, c), send_part.at[c], recv_part.at[v, c],
+            virt=inner,
+        )
+
     def back(k):
         return remote(
             psend.at[k], precv.at[k], back_sems.at[0, k], back_sems.at[1, k], blk=before
@@ -162,7 +176,7 @@
 
     def own_copy(make, send, c):
         return remote(
-            a_ref.at[c], make.at[v, c], send.at[v, c],
+            piece(a_ref, c), piece(make, v, c), send.at[v, c],
             (recv_part if make is part_full else recv_own).at[v, c],
             **({"blk": after} if make is part_full else {"virt": inner if send is send_in else outer}),
         )
@@ -185,18 +199,18 @@
 
     pl.semaphore_wait(barrier, 3 + middle.astype(jnp.int32))
 
-    for c in range(half):
+    for c in range(ahead):
         own_copy(own_full, send_in, c).start()
-    for c in range(half, occ):
+    for c in range(ahead, cuts):
         @pl.when(end)
         def _():
             own_copy(own_full, send_in, c).start()
-    for c in range(occ):
+    for c in range(cuts):
         @pl.when(middle)
         def _():
             own_copy(own_full, send_out, c).start()
     energy_copy.start()
-    for c in range(occ):
+    for c in range(cuts):
         own_copy(part_full, send_next, c).start()
     keep.start()
     for s in range(4):
@@ -231,7 +245,7 @@
         return source[s].reshape(size, aux)
 
     def part_arrives(s):
-        for c in range(occ):
+        for c in range(cuts):
             to_next(s, c).wait_recv()
 
     def pair_ratio(r, s, ratio_ref):
@@ -247,11 +261,9 @@
         pair_ratio(r, s, tu_ref)
         add_columns(total, tu_ref, own_full, s, first)
 
-    def cross(r, s, same):
-        if same:
-            part_arrives(s)
+    def cross(r, s, wait):
         k_ref[...] = contract(shard(part_full, r), shard(own_full, s))
-        if same is False:
+        if wait:
             part_arrives(s)
         x_ref[...] = contract(shard(own_full, r), shard(part_full, s))
         amplitudes(r, s)
@@ -272,13 +284,15 @@
     def from_outer(c):
         to_outer(outer, c).wait_recv()
         to_inner(outer, c).start()
-        to_next(outer, c).start()
-
-    def from_partner(c, forward):
+
+        @pl.when(even)
+        def _():
+            to_next(outer, c).start()
+
+    def from_partner(c):
         to_inner(inner, c).wait_recv()
         to_outer(inner, c).start()
-        if forward:
-            to_next(inner, c).start()
+        to_next(inner, c).start()
 
     def from_far(c):
         to_inner(far, c).wait_recv()
@@ -291,20 +305,28 @@
     diagonal(v, v, acc, True)
     energy_copy.wait_recv()
 
-    for c in range(half):
+    for c in range(occ):
         @pl.when(middle)
         def _():
             from_outer(c)
-            from_partner(c, False)
+            if c < ahead:
+                from_partner(c)
 
         @pl.when(end)
         def _():
             from_inner(inner, c)
 
-    cross(v, v, True)
+    part_arrives(v)
+
+    @pl.when(end & even)
+    def _():
+        for c in range(cuts):
+            part_to_inner(c).start()
+
+    cross(v, v, False)
     spread(v, True)
 
-    for c in range(half, occ):
+    for c in range(occ, cuts):
         @pl.when(middle)
         def _():
             from_outer(c)
@@ -315,34 +337,36 @@
 
     @pl.when(middle)
     def _():
-        for c in range(half, occ):
+        for c in range(ahead, cuts):
             own_copy(own_full, send_in, c).start()
-        for c in range(half):
+        for c in range(occ):
             from_far(c)
 
     diagonal(v, near, acc, False)
 
     @pl.when(middle)
     def _():
-        for c in range(half, occ - 1):
+        for c in range(occ, cuts - 1):
             from_far(c)
 
-    cross(v, near, False)
-    spread(near, False)
+    @pl.when(end)
+    def _():
+        cross(v, near, True)
+        spread(near, False)
 
     @pl.when(middle)
     def _():
-        from_far(occ - 1)
-        for c in range(half):
-            to_next(inner, c).start()
+        from_far(cuts - 1)
         pair_ratio(outer, far, td_ref)
-        cross(outer, far, False)
+        from_partner(ahead)
+        part_arrives(outer)
+        cross(outer, far, True)
+        from_partner(ahead + 1)
         for k in chunks:
             cols = slice(k * SEND_COLUMNS, (k + 1) * SEND_COLUMNS)
             hsend[k] = product(tu_ref, own_full, far, cols, SEND_COLUMNS).astype(jnp.bfloat16)
             help_back(k).start()
-        for c in range(half, occ - 1):
-            from_partner(c, True)
+        from_partner(ahead + 2)
 
         @pl.loop(0, aux // SUM_COLUMNS)
         def _(k):
@@ -351,23 +375,27 @@
                 t_ref, part_full, far, cols, SUM_COLUMNS
             )
 
+        for c in range(ahead + 3, cuts - 1):
+            from_partner(c)
         diagonal(v, far, acc, False)
-        from_partner(occ - 1, True)
+        from_partner(cuts - 1)
         for k in chunks:
             cols = slice(k * SEND_COLUMNS, (k + 1) * SEND_COLUMNS)
             help_back(k).wait_recv()
             rsend[k] = (racc[:, cols] + hrecv[k].astype(jnp.float32)).astype(jnp.bfloat16)
             result(k).start()
-        cross(v, far, None)
+        cross(v, outer, False)
+        spread(outer, False)
+        cross(v, far, False)
         spread(far, False)
 
     @pl.when(end)
     def _():
-        for c in range(occ):
+        for c in range(cuts):
             from_inner(far, c)
 
     diagonal(v, last, acc, False)
-    cross(v, last, False)
+    cross(v, last, True)
     for k in chunks:
         cols = slice(k * SEND_COLUMNS, (k + 1) * SEND_COLUMNS)
         psend[k] = (
@@ -395,17 +423,24 @@
     for k in chunks:
         back(k).wait_send()
         write(k).wait()
-    for c in range(occ):
+    for c in range(cuts):
         for s in (v, inner, far):
             to_next(s, c).wait_send()
         to_inner(v, c).wait_send()
 
         @pl.when(middle)
         def _():
-            to_next(outer, c).wait_send()
             to_inner(outer, c).wait_send()
             to_outer(v, c).wait_send()
             to_outer(inner, c).wait_send()
+
+        @pl.when(middle & even)
+        def _():
+            to_next(outer, c).wait_send()
+
+        @pl.when(end & even)
+        def _():
+            part_to_inner(c).wait_send()
 
     @pl.when(middle)
     def _():
@@ -438,7 +473,9 @@
             *[pltpu.VMEM((size, size), jnp.float32)] * 2,
             *[pltpu.VMEM((size, size), jnp.bfloat16)] * 3,
             pltpu.VMEM((parts, occ, rows, SEND_COLUMNS), jnp.bfloat16),
-            *[dma((members, occ))] * 5,
+            *[dma((members, 2 * occ))] * 3,
+            dma((2 * occ,)),
+            *[dma((members, 2 * occ))] * 2,
             *[dma((2, parts))] * 3,
             dma((2,)),
             dma((parts,)),
@@ -452,8 +489,8 @@
 
 def local(three_index, occ_energy, virt_energy):
     occ, rows, aux = three_index.shape
-    tiles = rows % 128 == 0 and aux % SUM_COLUMNS == 0 and occ % 2 == 0
-    if tiles and lax.axis_size("virt") == 4:
+    tiles = rows % 128 == 0 and aux % SUM_COLUMNS == 0 and occ >= 4
+    if tiles and lax.axis_size("virt") == 4 and lax.axis_size("blk") % 2 == 0:
         return fused_local(three_index, occ_energy, virt_energy)
     return plain_local(three_index, occ_energy, virt_energy)
 

time: 160 us -> 155 us (0.969)
  Pallas kernels: 156 us -> 152 us
    pallas_call x1, Pallas kernels: 156 us -> 152 us  [fused_local(): pl.pallas_call(functools.partial(kernel, blocks), out_shape=jax.ShapeDtyp...]
where the time goes in v4:
time: 155 us
  Pallas kernels  152 us (98%)
  local copies, waits for them, and re-layouts  3.16 us (2%)
    pallas_call x1, Pallas kernels, fused_local(): pl.pallas_call(functools.partial(kernel, blocks), out_shape=jax.ShapeDtyp...  152 us
    unnamed x1, local copies, waits for them, and re-layouts  3.16 us

profile of v4, /device:TPU:0, one launch (start us, length us, event | category | flops | bytes accessed | tf_op | source)
XLA Modules:
  0.0 154.9 jit_solution(4824815405934141500)
XLA Ops:
  0.0 151.7 %shard_map.37 = bf16[4,128,2048]{2,1,0:T(8,128)(2,1)} custom-call(bf16[4,128,2048]{2,1,0:T(8,128)(2,1)} %a_ref.1, f32[1,4]{1,0:T(1,128)} %bitcast.3, f32[4,1,128]{2,1,0:T(1,128)} %bitcast.2), custom_call_target="tpu_custom_call" | custom-call | tf_op jit(solution)/shard_map/pallas_call | solution.py:461
  151.7 3.2 %copy.5 = bf16[4,128,2048]{2,1,0:T(8,128)(2,1)} copy(bf16[4,128,2048]{2,1,0:T(8,128)(2,1)} %shard_map.37) | data formatting | bytes 4194304
